TPU v7x, 256 devices: a whole 4x4x8 slice. The times are simulated.
256 devices in a mesh: depth: 8 (over y, core), lat: 32 (over x, z).
Axes of the slice: x: 4, y: 4, z: 8, core: 2. Of those that a mesh axis runs over, the one named last changes fastest.
Arguments:
- volume: float32 [256, 512, 128], P('depth', 'lat'), may hold values from -6 to 6
Outputs:
- diffused: float32 [256, 512, 128], P('depth', 'lat')
All inputs are finite; a program needn't handle non-finite values.
Results may differ from a plain program's by a relative error of at most 0.0003.
Values sent between devices are 32-bit elements; how exact they have to be, the bound alone decides.
No kernel may reach another device: no remote copies, remote signals or barrier semaphores. Data moves between devices by JAX's collectives and lax.ppermute only.
A program may use at most 64 MiB of HBM per device.

v0:
```python
import jax
import jax.numpy as jnp
from jax import lax
from jax.sharding import PartitionSpec as P

TAU = 300.0
LAMBDA = 0.5


def with_halo(block, sides, width):
    for axis, dim in sides:
        count = lax.axis_size(axis)
        forward = [(i, i + 1) for i in range(count - 1)]
        backward = [(target, source) for source, target in forward]
        low = lax.ppermute(
            lax.slice_in_dim(block, block.shape[dim] - width, None, axis=dim), axis, forward
        )
        high = lax.ppermute(lax.slice_in_dim(block, 0, width, axis=dim), axis, backward)
        block = jnp.concatenate([low, block, high], axis=dim)
    return block


def conductance(diff):
    ratio = diff / LAMBDA
    return 1.0 / (1.0 + ratio * ratio)


def shifted(field, shift_by, axis, fill):
    length = field.shape[axis]
    widths = [(0, 0)] * field.ndim
    if shift_by > 0:
        widths[axis] = (shift_by, 0)
        padded = jnp.pad(field, widths, constant_values=fill)
        return lax.slice_in_dim(padded, 0, length, axis=axis)
    widths[axis] = (0, -shift_by)
    padded = jnp.pad(field, widths, constant_values=fill)
    return lax.slice_in_dim(padded, -shift_by, length - shift_by, axis=axis)


def smooth_padded(field, axis):
    return 0.25 * (shifted(field, 1, axis, 0.0) + 2.0 * field + shifted(field, -1, axis, 0.0))


def smooth_valid(field, axis):
    length = field.shape[axis]
    before = lax.slice_in_dim(field, 0, length - 2, axis=axis)
    middle = lax.slice_in_dim(field, 1, length - 1, axis=axis)
    after = lax.slice_in_dim(field, 2, length, axis=axis)
    return 0.25 * (before + 2.0 * middle + after)


def edge_mask(count, index, total, axis):
    edges = index * count + jnp.arange(count + 1, dtype=jnp.int32) - 1
    valid = jnp.logical_and(edges >= 0, edges <= count * total - 2).astype(jnp.float32)
    shape = [1, 1, 1]
    shape[axis] = count + 1
    return valid.reshape(shape)


def cyclic_solve(lower, diag, upper, sources, axis):
    length = diag.shape[axis]
    offset = 1
    while offset < length:
        low_prev = shifted(lower, offset, axis, 0.0)
        diag_prev = shifted(diag, offset, axis, 1.0)
        up_prev = shifted(upper, offset, axis, 0.0)
        low_next = shifted(lower, -offset, axis, 0.0)
        diag_next = shifted(diag, -offset, axis, 1.0)
        up_next = shifted(upper, -offset, axis, 0.0)
        left_factor = -lower / diag_prev
        right_factor = -upper / diag_next
        sources = tuple(
            (
                source
                + left_factor * shifted(source, offset, axis, 0.0)
                + right_factor * shifted(source, -offset, axis, 0.0)
                for source in sources
            )
        )
        diag = diag + left_factor * up_prev + right_factor * low_next
        lower = left_factor * low_prev
        upper = right_factor * up_next
        offset = offset * 2
    return tuple((source / diag for source in sources))


def line_coefficients(forward, axis):
    lower = -3.0 * TAU * shifted(forward, 1, axis, 0.0)
    upper = -3.0 * TAU * forward
    return (lower, 1.0 - lower - upper, upper)


def local_spike(edges, field, axis):
    count = field.shape[axis]
    inner_lower = -3.0 * TAU * lax.slice_in_dim(edges, 0, count, axis=axis)
    inner_upper = -3.0 * TAU * lax.slice_in_dim(edges, 1, count + 1, axis=axis)
    diag = 1.0 - inner_lower - inner_upper
    shape = [1, 1, 1]
    shape[axis] = count
    position = jnp.arange(count, dtype=jnp.int32).reshape(shape)
    is_first = position == 0
    is_last = position == count - 1
    lower = jnp.where(is_first, 0.0, inner_lower)
    upper = jnp.where(is_last, 0.0, inner_upper)
    left_source = jnp.where(is_first, inner_lower, 0.0)
    right_source = jnp.where(is_last, inner_upper, 0.0)
    particular, left_spike, right_spike = cyclic_solve(
        lower, diag, upper, (field, left_source, right_source), axis
    )
    ends = []
    for solved in (particular, left_spike, right_spike):
        ends.append(lax.index_in_dim(solved, 0, axis, keepdims=False))
        ends.append(lax.index_in_dim(solved, count - 1, axis, keepdims=False))
    return (particular, left_spike, right_spike, jnp.stack(ends, axis=0)[None])


def reduced_solve(gathered):

    def sweep_down(carry, block):
        chain_prev, carry_last = carry
        first_val = block[0]
        last_val = block[1]
        left_first = block[2]
        left_last = block[3]
        right_first = block[4]
        right_last = block[5]
        pivot = 1.0 - left_first * chain_prev
        result_first = (first_val - left_first * carry_last) / pivot
        result_last = last_val - left_last * carry_last + left_last * chain_prev * result_first
        factor_first = right_first / pivot
        chain_new = right_last + left_last * chain_prev * factor_first
        return ((chain_new, result_last), (factor_first, chain_new, result_first, result_last))

    zero_lines = jnp.zeros_like(gathered[0, 0])
    _, factors = lax.scan(sweep_down, (zero_lines, zero_lines), gathered)

    def sweep_up(first_later, block):
        factor_first, chain_new, result_first, result_last = block
        first_here = result_first - factor_first * first_later
        last_here = result_last - chain_new * first_later
        return (first_here, (first_here, last_here))

    _, (firsts, lasts) = lax.scan(sweep_up, zero_lines, factors, reverse=True)
    return (firsts, lasts)


def spike_finish(particular, left_spike, right_spike, firsts, lasts, index, total, axis):
    last_prev = lax.dynamic_index_in_dim(lasts, jnp.maximum(index - 1, 0), 0, keepdims=False)
    first_next = lax.dynamic_index_in_dim(
        firsts, jnp.minimum(index + 1, total - 1), 0, keepdims=False
    )
    return (
        particular
        - left_spike * jnp.expand_dims(last_prev, axis)
        - right_spike * jnp.expand_dims(first_next, axis)
    )


def shards(volume):
    depth_total = lax.axis_size("depth")
    depth_index = lax.axis_index("depth")
    lat_total = lax.axis_size("lat")
    lat_index = lax.axis_index("lat")
    planes, rows, columns = volume.shape
    padded = with_halo(volume, (("depth", 0), ("lat", 1)), 2)
    smoothed = smooth_padded(padded, 2)
    smoothed = smooth_valid(smoothed, 1)
    smoothed = smooth_valid(smoothed, 0)
    core = smoothed[1:-1, 1:-1]
    cond_x = jnp.pad(conductance(core[:, :, 1:] - core[:, :, :-1]), ((0, 0), (0, 0), (0, 1)))
    band_y = smoothed[1:-1]
    cond_y = conductance(band_y[:, 1:] - band_y[:, :-1]) * edge_mask(rows, lat_index, lat_total, 1)
    band_z = smoothed[:, 1:-1]
    cond_z = conductance(band_z[1:] - band_z[:-1]) * edge_mask(planes, depth_index, depth_total, 0)
    lower_x, diag_x, upper_x = line_coefficients(cond_x, 2)
    (solved_x,) = cyclic_solve(lower_x, diag_x, upper_x, (volume,), 2)
    field = lax.all_to_all(volume, "lat", split_axis=2, concat_axis=1, tiled=True)
    forward = lax.all_to_all(cond_y[:, 1:], "lat", split_axis=2, concat_axis=1, tiled=True)
    count, length, width = field.shape
    flat_field = jnp.transpose(field, (1, 0, 2)).reshape(length, count * width)
    flat_forward = jnp.transpose(forward, (1, 0, 2)).reshape(length, count * width)
    lower, diag, upper = line_coefficients(flat_forward, 0)
    (solved,) = cyclic_solve(lower, diag, upper, (flat_field,), 0)
    returned = jnp.transpose(solved.reshape(length, count, width), (1, 0, 2))
    solved_y = lax.all_to_all(returned, "lat", split_axis=1, concat_axis=2, tiled=True)
    part_z, left_z, right_z, ends_z = local_spike(cond_z, volume, 0)
    gathered_z = lax.all_gather(ends_z, "depth", axis=0, tiled=True)
    firsts_z, lasts_z = reduced_solve(gathered_z)
    solved_z = spike_finish(part_z, left_z, right_z, firsts_z, lasts_z, depth_index, depth_total, 0)
    return (solved_x + solved_y + solved_z) / 3.0


def solution(mesh):
    placed = (P("depth", "lat", None),)
    return jax.shard_map(
        shards, mesh=mesh, in_specs=placed, out_specs=P("depth", "lat", None), check_vma=False
    )
```

profile of v0, /device:TPU:32, one launch (start us, length us, event | category | flops | bytes accessed | tf_op | source)
XLA Modules:
  0.0 110.6 jit_solution(14266920727948924884)
XLA Ops:
  0.0 0.7 fusion.377
  0.7 1.3 %collective-permute-start.1 = (f32[2,16,128]{2,1,0:T(8,128)S(1)}, f32[2,16,128]{2,1,0:T(8,128)S(1)}, u32[]{:S(2)}, u32[]{:S(2)}) collective-permute-start(f32[2,16,128]{2,1,0:T(8,128)S(1)} %get-tuple-element.424), channel_id=1, source_target_pairs={{32,0},{64,32},{96,64},{128,96},{160,128},{192,160},{224,192},{33,... | collective-permute-start | bytes 49160 | tf_op jit(solution)/shard_map/ppermute | solution.py:18
  2.0 3.0 %collective-permute-start = (f32[2,16,128]{2,1,0:T(8,128)S(1)}, f32[2,16,128]{2,1,0:T(8,128)S(1)}, u32[]{:S(2)}, u32[]{:S(2)}) collective-permute-start(f32[2,16,128]{2,1,0:T(8,128)S(1)} %get-tuple-element.423), channel_id=1, source_target_pairs={{0,32},{32,64},{64,96},{96,128},{128,160},{160,192},{192,224},{1,3... | collective-permute-start | bytes 49160 | tf_op jit(solution)/shard_map/ppermute | solution.py:15
  5.1 1.5 %copy.156 = f32[32,16,128]{0,1,2:T(8,128)S(1)} copy(f32[32,16,128]{2,1,0:T(8,128)} %param.5) | data formatting | bytes 524288 | tf_op args[0]
  6.5 1.2 %reshape.56 = f32[32,1,2048]{2,1,0:T(1,128)} reshape(f32[128,16,32]{2,1,0:T(8,128)S(1)} %bitcast.134) | data formatting | bytes 524288
  7.7 11.3 %all-to-all-start = ((f32[32,1,2048]{2,1,0:T(1,128)}), f32[32,1,2048]{2,1,0:T(1,128)S(1)}, u32[]{:S(2)}, u32[]{:S(2)}) async-start(f32[32,1,2048]{2,1,0:T(1,128)} %reshape.56), calls=%async_computation | async-start | bytes 524288 | tf_op jit(solution)/shard_map/all_to_all | solution.py:177
  19.2 3.4 %collective-permute-start.2 = (f32[36,2,128]{2,0,1:T(8,128)S(1)}, f32[36,2,128]{2,0,1:T(8,128)S(1)}, u32[]{:S(2)}, u32[]{:S(2)}) collective-permute-start(f32[36,2,128]{2,0,1:T(8,128)S(1)} %copy.177), channel_id=1, source_target_pairs={{0,1},{1,2},{2,3},{3,4},{4,5},{5,6},{6,7},{7,8},{8,9},{9,10},{10,1... | collective-permute-start | bytes 110600 | tf_op jit(solution)/shard_map/ppermute | solution.py:15
  22.8 2.5 %collective-permute-start.3 = (f32[36,2,128]{2,0,1:T(8,128)S(1)}, f32[36,2,128]{2,0,1:T(8,128)S(1)}, u32[]{:S(2)}, u32[]{:S(2)}) collective-permute-start(f32[36,2,128]{2,0,1:T(8,128)S(1)} %copy.178), channel_id=1, source_target_pairs={{1,0},{2,1},{3,2},{4,3},{5,4},{6,5},{7,6},{8,7},{9,8},{10,9},{11,1... | collective-permute-start | bytes 110600 | tf_op jit(solution)/shard_map/ppermute | solution.py:18
  25.3 1.8 %collective-permute-done.2 = f32[36,2,128]{2,0,1:T(8,128)S(1)} collective-permute-done((f32[36,2,128]{2,0,1:T(8,128)S(1)}, f32[36,2,128]{2,0,1:T(8,128)S(1)}, u32[]{:S(2)}, u32[]{:S(2)}) %collective-permute-start.2) | collective-permute-done | bytes 36896 | tf_op jit(solution)/shard_map/ppermute | solution.py:15
  27.2 1.8 %collective-permute-done.3 = f32[36,2,128]{2,0,1:T(8,128)S(1)} collective-permute-done((f32[36,2,128]{2,0,1:T(8,128)S(1)}, f32[36,2,128]{2,0,1:T(8,128)S(1)}, u32[]{:S(2)}, u32[]{:S(2)}) %collective-permute-start.3) | collective-permute-done | bytes 36896 | tf_op jit(solution)/shard_map/ppermute | solution.py:18
  29.8 0.5 copy.159
  30.3 1.2 %reshape.58 = f32[32,1,2048]{2,1,0:T(1,128)} reshape(f32[128,16,32]{2,1,0:T(8,128)S(1)} %bitcast.132) | data formatting | bytes 524288
  31.8 0.3 fusion.167
  32.1 0.3 fusion.120
  34.5 13.4 %all-gather = f32[48,16,128]{2,1,0:T(8,128)S(1)} all-gather(f32[6,16,128]{2,1,0:T(8,128)S(1)} %constant_dynamic-update-slice_fusion.3), channel_id=2, replica_groups=mesh['depth'=8,'lat'=32] {'depth'}, dimensions={0}, use_global_device_ids=true | all-gather | bytes 442368 | tf_op jit(solution)/shard_map/all_gather | solution.py:187
  47.9 0.4 while.40
  48.4 0.3 while.41
  48.7 0.7 fusion.239
  49.5 0.7 fusion.244
  50.2 0.3 fusion.251
  50.5 0.6 fusion.256
  51.1 0.3 fusion.263
  51.5 0.6 fusion.268
  52.1 0.3 fusion.275
  52.5 0.7 copy-done.6
  53.2 10.0 %all-to-all-start.1 = ((f32[32,1,2048]{2,1,0:T(1,128)}), f32[32,1,2048]{2,1,0:T(1,128)}, u32[]{:S(2)}, u32[]{:S(2)}) async-start(f32[32,1,2048]{2,1,0:T(1,128)} %reshape.58), calls=%async_computation.1 | async-start | bytes 524288 | tf_op jit(solution)/shard_map/all_to_all | solution.py:178
  63.2 1.3 %fusion.280 = (f32[32,16,128]{2,0,1:T(8,128)}, f32[32,16,128]{2,0,1:T(8,128)S(1)}, f32[32,16,128]{2,0,1:T(8,128)S(1)}) fusion(f32[32,16,128]{2,0,1:T(8,128)S(1)} %get-tuple-element.323, f32[32,16,128]{2,0,1:T(8,128)S(1)} %fusion.275, f32[32,16,128]{2,0,1:T(8,128)S(1)} %get-tuple-element.324, f32[32,16,128]{2,0,1:T(8,128)S(1)} %fusion.263, ...), kind=kLoop, calls=%fused_computation.488 | loop fusion | flops 917504 | bytes 2097152 | tf_op jit(solution)/shard_map/add | solution.py:74
  64.5 0.3 fusion.287
  64.8 0.5 broadcast.603
  65.4 1.2 %reduce.1 = f32[32,2048]{1,0:T(8,128)S(1)} reduce(f32[32,1,2048]{2,1,0:T(1,128)S(1)} %copy-done.7, f32[]{:T(128)} %broadcast.603), dimensions={1}, to_apply=%all_to_all.39.reduce_sub_computation | reduce | bytes 524292 | tf_op jit(solution)/shard_map/all_to_all | solution.py:177
  66.6 0.3 reshape.57
  67.0 0.3 copy.158
  67.4 0.8 reshape.52
  68.2 7.8 %all-to-all-done.1 = f32[32,1,2048]{2,1,0:T(1,128)} async-done(((f32[32,1,2048]{2,1,0:T(1,128)}), f32[32,1,2048]{2,1,0:T(1,128)}, u32[]{:S(2)}, u32[]{:S(2)}) %all-to-all-start.1) | async-done | bytes 262176 | tf_op jit(solution)/shard_map/all_to_all | solution.py:178
  76.0 2.1 %reduce = f32[32,2048]{1,0:T(8,128)S(1)} reduce(f32[32,1,2048]{2,1,0:T(1,128)} %all-to-all-done.1, f32[]{:T(128)} %broadcast.603), dimensions={1}, to_apply=%all_to_all.43.reduce_sub_computation | reduce | bytes 524292 | tf_op jit(solution)/shard_map/all_to_all | solution.py:178
  78.1 0.3 reshape.59
  78.6 0.3 copy.161
  79.2 0.7 copy-done.5
  80.0 0.8 fusion.30
  80.7 0.7 fusion.35
  81.4 0.3 fusion.42
  81.8 0.6 fusion.47
  82.4 0.3 fusion.54
  82.8 0.6 fusion.59
  83.4 0.3 fusion.66
  83.7 0.6 fusion.71
  84.4 0.3 fusion.78
  84.7 0.6 fusion.83
  85.3 0.3 fusion.90
  85.7 0.6 fusion.95
  86.3 0.3 fusion.102
  86.7 0.4 fusion.107
  87.4 0.4 copy.162
  87.8 1.4 %reshape.60 = f32[32,1,2048]{2,1,0:T(1,128)} reshape(f32[512,4,32]{2,1,0:T(4,128)S(1)} %bitcast.133) | data formatting | bytes 524288
  89.2 4.9 %all-to-all-start.2 = ((f32[32,1,2048]{2,1,0:T(1,128)}), f32[32,1,2048]{2,1,0:T(1,128)S(1)}, u32[]{:S(2)}, u32[]{:S(2)}) async-start(f32[32,1,2048]{2,1,0:T(1,128)} %reshape.60), calls=%async_computation.2 | async-start | bytes 524288 | tf_op jit(solution)/shard_map/all_to_all | solution.py:185
  94.1 1.3 %fusion.292 = (f32[32,16,128]{2,0,1:T(8,128)}, f32[32,16,128]{2,0,1:T(8,128)S(1)}, f32[32,16,128]{2,0,1:T(8,128)S(1)}) fusion(f32[32,16,128]{2,0,1:T(8,128)S(1)} %copy-done.9, f32[32,16,128]{2,0,1:T(8,128)S(1)} %fusion.287, f32[32,16,128]{2,0,1:T(8,128)S(1)} %get-tuple-element.321, f32[32,16,128]{2,0,1:T(8,128)S(1)} %fusion.275, ...), kind=kLoop, calls=%fused_computation.500 | loop fusion | flops 917504 | bytes 2097152 | tf_op jit(solution)/shard_map/add | solution.py:74
  95.4 0.6 fusion.308
  96.1 10.1 %all-to-all-done.2 = f32[32,1,2048]{2,1,0:T(1,128)S(1)} async-done(((f32[32,1,2048]{2,1,0:T(1,128)}), f32[32,1,2048]{2,1,0:T(1,128)S(1)}, u32[]{:S(2)}, u32[]{:S(2)}) %all-to-all-start.2) | async-done | bytes 262176 | tf_op jit(solution)/shard_map/all_to_all | solution.py:185
  106.2 1.2 %reduce.2 = f32[32,2048]{1,0:T(8,128)S(1)} reduce(f32[32,1,2048]{2,1,0:T(1,128)S(1)} %all-to-all-done.2, f32[]{:T(128)} %broadcast.603), dimensions={1}, to_apply=%all_to_all.47.reduce_sub_computation | reduce | bytes 524292 | tf_op jit(solution)/shard_map/all_to_all | solution.py:185
  107.4 0.5 reshape.61
  108.2 0.4 copy.165
  108.6 0.5 copy-done.2
  109.2 0.5 fusion.324
  109.7 0.9 copy.175
  (95 shorter events, 5.1 us)
Async XLA Ops:
  0.7 18.3 %collective-permute-start.1 = (f32[2,16,128]{2,1,0:T(8,128)S(1)}, f32[2,16,128]{2,1,0:T(8,128)S(1)}, u32[]{:S(2)}, u32[]{:S(2)}) collective-permute-start(f32[2,16,128]{2,1,0:T(8,128)S(1)} %get-tuple-element.424), channel_id=1, source_target_pairs={{32,0},{64,32},{96,64},{128,96},{160,128},{192,160},{224,192},{33,... | collective-permute-start | bytes 49160 | tf_op jit(solution)/shard_map/ppermute | solution.py:18
  2.0 17.1 %collective-permute-start = (f32[2,16,128]{2,1,0:T(8,128)S(1)}, f32[2,16,128]{2,1,0:T(8,128)S(1)}, u32[]{:S(2)}, u32[]{:S(2)}) collective-permute-start(f32[2,16,128]{2,1,0:T(8,128)S(1)} %get-tuple-element.423), channel_id=1, source_target_pairs={{0,32},{32,64},{64,96},{96,128},{128,160},{160,192},{192,224},{1,3... | collective-permute-start | bytes 49160 | tf_op jit(solution)/shard_map/ppermute | solution.py:15
  7.7 11.4 %copy-start = (f32[32,16,128]{2,1,0:T(8,128)S(1)}, f32[32,16,128]{2,1,0:T(8,128)}, u32[]{:S(2)}) copy-start(f32[32,16,128]{2,1,0:T(8,128)} %param.5) | copy-start | bytes 786436
  7.7 44.8 %all-to-all-start = ((f32[32,1,2048]{2,1,0:T(1,128)}), f32[32,1,2048]{2,1,0:T(1,128)S(1)}, u32[]{:S(2)}, u32[]{:S(2)}) async-start(f32[32,1,2048]{2,1,0:T(1,128)} %reshape.56), calls=%async_computation | async-start | bytes 524288 | tf_op jit(solution)/shard_map/all_to_all | solution.py:177
  19.2 7.9 %collective-permute-start.2 = (f32[36,2,128]{2,0,1:T(8,128)S(1)}, f32[36,2,128]{2,0,1:T(8,128)S(1)}, u32[]{:S(2)}, u32[]{:S(2)}) collective-permute-start(f32[36,2,128]{2,0,1:T(8,128)S(1)} %copy.177), channel_id=1, source_target_pairs={{0,1},{1,2},{2,3},{3,4},{4,5},{5,6},{6,7},{7,8},{8,9},{9,10},{10,1... | collective-permute-start | bytes 110600 | tf_op jit(solution)/shard_map/ppermute | solution.py:15
  22.8 6.2 %collective-permute-start.3 = (f32[36,2,128]{2,0,1:T(8,128)S(1)}, f32[36,2,128]{2,0,1:T(8,128)S(1)}, u32[]{:S(2)}, u32[]{:S(2)}) collective-permute-start(f32[36,2,128]{2,0,1:T(8,128)S(1)} %copy.178), channel_id=1, source_target_pairs={{1,0},{2,1},{3,2},{4,3},{5,4},{6,5},{7,6},{8,7},{9,8},{10,9},{11,1... | collective-permute-start | bytes 110600 | tf_op jit(solution)/shard_map/ppermute | solution.py:18
  34.4 13.5 %copy-start.1 = (f32[32,16,128]{2,0,1:T(8,128)}, f32[32,16,128]{2,0,1:T(8,128)S(1)}, u32[]{:S(2)}) copy-start(f32[32,16,128]{2,0,1:T(8,128)S(1)} %get-tuple-element.380) | copy-start | bytes 786436
  34.4 13.5 %copy-start.3 = (f32[32,16,128]{2,0,1:T(8,128)}, f32[32,16,128]{2,0,1:T(8,128)S(1)}, u32[]{:S(2)}) copy-start(f32[32,16,128]{2,0,1:T(8,128)S(1)} %get-tuple-element.381) | copy-start | bytes 786436
  52.5 0.7 copy-start.6
  53.2 22.8 %all-to-all-start.1 = ((f32[32,1,2048]{2,1,0:T(1,128)}), f32[32,1,2048]{2,1,0:T(1,128)}, u32[]{:S(2)}, u32[]{:S(2)}) async-start(f32[32,1,2048]{2,1,0:T(1,128)} %reshape.58), calls=%async_computation.1 | async-start | bytes 524288 | tf_op jit(solution)/shard_map/all_to_all | solution.py:178
  64.5 0.9 copy-start.7
  79.0 1.0 copy-start.5
  89.2 4.9 %copy-start.9 = (f32[32,16,128]{2,0,1:T(8,128)S(1)}, f32[32,16,128]{2,0,1:T(8,128)}, u32[]{:S(2)}) copy-start(f32[32,16,128]{2,0,1:T(8,128)} %get-tuple-element.320) | copy-start | bytes 786436
  89.2 17.0 %all-to-all-start.2 = ((f32[32,1,2048]{2,1,0:T(1,128)}), f32[32,1,2048]{2,1,0:T(1,128)S(1)}, u32[]{:S(2)}, u32[]{:S(2)}) async-start(f32[32,1,2048]{2,1,0:T(1,128)} %reshape.60), calls=%async_computation.2 | async-start | bytes 524288 | tf_op jit(solution)/shard_map/all_to_all | solution.py:185
  108.1 1.0 copy-start.2
  108.1 1.0 copy-start.4
  108.1 1.1 copy-start.8
where the time goes:
time: 111 us
  starting transfers between devices  36.4 us (33%)
  other arithmetic  23.5 us (21%)
  waiting for transfers between devices  21.6 us (19%)
  local copies, waits for them, and re-layouts  14.5 us (13%)
  blocking collectives  13.4 us (12%)
    all_gather x1, blocking collectives, shards(): gathered_z = lax.all_gather(ends_z, 'depth', axis=0, tiled=True)  13.4 us
    all_to_all x1, starting transfers between devices, shards(): lax.all_to_all(volume, 'lat', split_axis=2, concat_axis=1, tiled=True)  11.3 us
    add x20, other arithmetic, cyclic_solve(): source + left_factor * shifted(source, offset, axis, 0.0)  10.9 us
    all_to_all x1, waiting for transfers between devices, shards(): lax.all_to_all(returned, 'lat', split_axis=1, concat_axis=2, tiled=True)  10.1 us
    all_to_all x1, starting transfers between devices, shards(): lax.all_to_all(cond_y[:, 1:], 'lat', split_axis=2, concat_axis=1, tiled=T...  9.98 us
    unnamed x37, local copies, waits for them, and re-layouts  8.81 us
    all_to_all x1, waiting for transfers between devices, shards(): lax.all_to_all(cond_y[:, 1:], 'lat', split_axis=2, concat_axis=1, tiled=T...  7.83 us
    ppermute x2, starting transfers between devices, with_halo(): lax.ppermute(lax.slice_in_dim(block, block.shape[dim] - width, None, axis...  6.4 us
  transfers between devices with their start and end apart: 7, of which 4 were waited for; matrix products, arithmetic and copies ran while one was open for 17% of the time, Pallas kernels for 0%

commit v1 on v0

--- a/solution.py
+++ b/solution.py
@@ -184,7 +184,30 @@
     returned = jnp.transpose(solved.reshape(length, count, width), (1, 0, 2))
     solved_y = lax.all_to_all(returned, "lat", split_axis=1, concat_axis=2, tiled=True)
     part_z, left_z, right_z, ends_z = local_spike(cond_z, volume, 0)
-    gathered_z = lax.all_gather(ends_z, "depth", axis=0, tiled=True)
+    all_rows, tmp, n_now = (
+        jax.lax.axis_size("depth"),
+        jax.lax.axis_index("depth"),
+        ends_z.shape[0],
+    )
+    panels = [num * all_rows if b == 0 else num for b, num in enumerate(ends_z.shape)]
+    gathered_z = lax.dynamic_update_slice_in_dim(
+        jnp.zeros(panels, ends_z.dtype), ends_z, tmp * n_now, axis=0
+    )
+    t_next = big = ends_z
+    it = 1
+    while it < all_rows // 2 + 1:
+        t_next = jax.lax.ppermute(
+            t_next, "depth", [(b, (b + 1) % all_rows) for b in range(all_rows)]
+        )
+        gathered_z = lax.dynamic_update_slice_in_dim(
+            gathered_z, t_next, (tmp - it) % all_rows * n_now, axis=0
+        )
+        if 2 * it < all_rows:
+            big = jax.lax.ppermute(big, "depth", [(b, (b - 1) % all_rows) for b in range(all_rows)])
+            gathered_z = lax.dynamic_update_slice_in_dim(
+                gathered_z, big, (tmp + it) % all_rows * n_now, axis=0
+            )
+        it = it + 1
     firsts_z, lasts_z = reduced_solve(gathered_z)
     solved_z = spike_finish(part_z, left_z, right_z, firsts_z, lasts_z, depth_index, depth_total, 0)
     return (solved_x + solved_y + solved_z) / 3.0

time: 111 us -> 113 us (1.018); the launches traced: 111 us -> 111 us
  blocking collectives: 13.4 us -> 0 us
  starting transfers between devices: 36.4 us -> 44.6 us
  other arithmetic: 23.5 us -> 28.4 us
  waiting for transfers between devices: 21.6 us -> 24.8 us
  local copies, waits for them, and re-layouts: 14.5 us -> 12.5 us
    all_gather x1 -> x0, blocking collectives: 13.4 us -> none  [shards(): gathered_z = lax.all_gather(ends_z, 'depth', axis=0, tiled=True)]
    ppermute x0 -> x7, starting transfers between devices: none -> 8.88 us  [the longest x3 8.85 us: shards(): jax.lax.ppermute(big, 'depth', [(b, (b - 1) % all_rows) for b in range(al...]
    ppermute x0 -> x7, waiting for transfers between devices: none -> 8.19 us  [the longest x4 8.18 us: shards(): jax.lax.ppermute(t_next, 'depth', [(b, (b + 1) % all_rows) for b in range...]
    dynamic_update_slice x16, other arithmetic: 0.36 us -> 6.03 us  [reduced_solve(): _, factors = lax.scan(sweep_down, (zero_lines, zero_lines), gathered)]
    all_to_all x1, waiting for transfers between devices: 10.1 us -> 5.12 us  [shards(): lax.all_to_all(returned, 'lat', split_axis=1, concat_axis=2, tiled=True)]
    unnamed x37 -> x31, local copies, waits for them, and re-layouts: 8.81 us -> 7.32 us
  transfers between devices with their start and end apart: 7 -> 14, of which waited for: 4 -> 7; matrix products, arithmetic and copies ran while one was open for 17% -> 22% of each run, Pallas kernels for 0% -> 0%
where the time goes in v1:
time: 113 us; the launch traced here: 111 us
  starting transfers between devices  44.6 us (39%)
  other arithmetic  28.4 us (25%)
  waiting for transfers between devices  24.8 us (22%)
  local copies, waits for them, and re-layouts  12.5 us (11%)
    all_to_all x1, starting transfers between devices, shards(): lax.all_to_all(volume, 'lat', split_axis=2, concat_axis=1, tiled=True)  11.3 us
    add x20, other arithmetic, cyclic_solve(): source + left_factor * shifted(source, offset, axis, 0.0)  10.1 us
    all_to_all x1, starting transfers between devices, shards(): lax.all_to_all(cond_y[:, 1:], 'lat', split_axis=2, concat_axis=1, tiled=T...  9.79 us
    ppermute x3, starting transfers between devices, shards(): jax.lax.ppermute(big, 'depth', [(b, (b - 1) % all_rows) for b in range(al...  8.85 us
    ppermute x4, waiting for transfers between devices, shards(): jax.lax.ppermute(t_next, 'depth', [(b, (b + 1) % all_rows) for b in range...  8.18 us
    all_to_all x1, waiting for transfers between devices, shards(): lax.all_to_all(cond_y[:, 1:], 'lat', split_axis=2, concat_axis=1, tiled=T...  7.82 us
    unnamed x31, local copies, waits for them, and re-layouts  7.32 us
    ppermute x2, starting transfers between devices, with_halo(): lax.ppermute(lax.slice_in_dim(block, block.shape[dim] - width, None, axis...  6.4 us
  transfers between devices with their start and end apart: 14, of which 7 were waited for; matrix products, arithmetic and copies ran while one was open for 22% of the time, Pallas kernels for 0%

profile of v1, /device:TPU:32, one launch (start us, length us, event | category | flops | bytes accessed | tf_op | source)
XLA Modules:
  0.0 111.5 jit_solution(12969237860602051372)
XLA Ops:
  0.0 0.7 fusion.377
  0.7 1.3 %collective-permute-start.1 = (f32[2,16,128]{2,1,0:T(8,128)S(1)}, f32[2,16,128]{2,1,0:T(8,128)S(1)}, u32[]{:S(2)}, u32[]{:S(2)}) collective-permute-start(f32[2,16,128]{2,1,0:T(8,128)S(1)} %get-tuple-element.416), channel_id=1, source_target_pairs={{32,0},{64,32},{96,64},{128,96},{160,128},{192,160},{224,192},{33,... | collective-permute-start | bytes 49160 | tf_op jit(solution)/shard_map/ppermute | solution.py:18
  2.0 3.0 %collective-permute-start = (f32[2,16,128]{2,1,0:T(8,128)S(1)}, f32[2,16,128]{2,1,0:T(8,128)S(1)}, u32[]{:S(2)}, u32[]{:S(2)}) collective-permute-start(f32[2,16,128]{2,1,0:T(8,128)S(1)} %get-tuple-element.415), channel_id=1, source_target_pairs={{0,32},{32,64},{64,96},{96,128},{128,160},{160,192},{192,224},{1,3... | collective-permute-start | bytes 49160 | tf_op jit(solution)/shard_map/ppermute | solution.py:15
  5.1 1.5 %copy.170 = f32[32,16,128]{0,1,2:T(8,128)S(1)} copy(f32[32,16,128]{2,1,0:T(8,128)} %param.5) | data formatting | bytes 524288 | tf_op args[0]
  6.5 1.2 %reshape.55 = f32[32,1,2048]{2,1,0:T(1,128)} reshape(f32[128,16,32]{2,1,0:T(8,128)S(1)} %bitcast.135) | data formatting | bytes 524288
  7.7 11.3 %all-to-all-start = ((f32[32,1,2048]{2,1,0:T(1,128)}), f32[32,1,2048]{2,1,0:T(1,128)S(1)}, u32[]{:S(2)}, u32[]{:S(2)}) async-start(f32[32,1,2048]{2,1,0:T(1,128)} %reshape.55), calls=%async_computation | async-start | bytes 524288 | tf_op jit(solution)/shard_map/all_to_all | solution.py:177
  19.2 3.4 %collective-permute-start.2 = (f32[36,2,128]{2,0,1:T(8,128)S(1)}, f32[36,2,128]{2,0,1:T(8,128)S(1)}, u32[]{:S(2)}, u32[]{:S(2)}) collective-permute-start(f32[36,2,128]{2,0,1:T(8,128)S(1)} %copy.191), channel_id=1, source_target_pairs={{0,1},{1,2},{2,3},{3,4},{4,5},{5,6},{6,7},{7,8},{8,9},{9,10},{10,1... | collective-permute-start | bytes 110600 | tf_op jit(solution)/shard_map/ppermute | solution.py:15
  22.9 2.5 %collective-permute-start.3 = (f32[36,2,128]{2,0,1:T(8,128)S(1)}, f32[36,2,128]{2,0,1:T(8,128)S(1)}, u32[]{:S(2)}, u32[]{:S(2)}) collective-permute-start(f32[36,2,128]{2,0,1:T(8,128)S(1)} %copy.192), channel_id=1, source_target_pairs={{1,0},{2,1},{3,2},{4,3},{5,4},{6,5},{7,6},{8,7},{9,8},{10,9},{11,1... | collective-permute-start | bytes 110600 | tf_op jit(solution)/shard_map/ppermute | solution.py:18
  25.4 1.7 %collective-permute-done.2 = f32[36,2,128]{2,0,1:T(8,128)S(1)} collective-permute-done((f32[36,2,128]{2,0,1:T(8,128)S(1)}, f32[36,2,128]{2,0,1:T(8,128)S(1)}, u32[]{:S(2)}, u32[]{:S(2)}) %collective-permute-start.2) | collective-permute-done | bytes 36896 | tf_op jit(solution)/shard_map/ppermute | solution.py:15
  27.2 1.9 %collective-permute-done.3 = f32[36,2,128]{2,0,1:T(8,128)S(1)} collective-permute-done((f32[36,2,128]{2,0,1:T(8,128)S(1)}, f32[36,2,128]{2,0,1:T(8,128)S(1)}, u32[]{:S(2)}, u32[]{:S(2)}) %collective-permute-start.3) | collective-permute-done | bytes 36896 | tf_op jit(solution)/shard_map/ppermute | solution.py:18
  32.7 2.9 %collective-permute-start.5 = (f32[1,6,16,128]{3,2,1,0:T(8,128)S(1)}, f32[1,6,16,128]{3,2,1,0:T(8,128)S(1)}, u32[]{:S(2)}, u32[]{:S(2)}) collective-permute-start(f32[1,6,16,128]{3,2,1,0:T(8,128)S(1)} %bitcast.145), channel_id=1, source_target_pairs={{0,224},{32,0},{64,32},{96,64},{128,96},{160,128},{192,160},{224,1... | collective-permute-start | bytes 147464 | tf_op jit(solution)/shard_map/ppermute | solution.py:206
  35.8 0.7 fusion.239
  36.6 0.7 fusion.244
  37.6 0.6 fusion.256
  38.6 0.6 fusion.268
  39.5 0.6 fusion.280
  40.5 1.3 %fusion.292 = (f32[32,16,128]{2,0,1:T(8,128)}, f32[32,16,128]{2,0,1:T(8,128)S(1)}, f32[32,16,128]{2,0,1:T(8,128)S(1)}) fusion(f32[32,16,128]{2,0,1:T(8,128)S(1)} %get-tuple-element.312, f32[32,16,128]{2,0,1:T(8,128)S(1)} %fusion.287, f32[32,16,128]{2,0,1:T(8,128)S(1)} %get-tuple-element.313, f32[32,16,128]{2,0,1:T(8,128)S(1)} %fusion.275, ...), kind=kLoop, calls=%fused_computation.500 | loop fusion | flops 917504 | bytes 2097152 | tf_op jit(solution)/shard_map/add | solution.py:74
  41.8 1.5 %fusion.308 = (f32[32,16,128]{2,0,1:T(8,128)}, f32[32,16,128]{2,0,1:T(8,128)}, f32[32,16,128]{2,0,1:T(8,128)}) fusion(f32[32,16,128]{2,0,1:T(8,128)S(1)} %get-tuple-element.310, f32[32,16,128]{2,0,1:T(8,128)S(1)} %fusion.287, f32[32,16,128]{2,0,1:T(8,128)S(1)} %get-tuple-element.311), kind=kLoop, calls=%fused_computation.516 | loop fusion | flops 786432 | bytes 1572864 | tf_op jit(solution)/shard_map/mul | solution.py:82
  43.5 0.5 copy.173
  44.0 1.2 %reshape.57 = f32[32,1,2048]{2,1,0:T(1,128)} reshape(f32[128,16,32]{2,1,0:T(8,128)S(1)} %bitcast.133) | data formatting | bytes 524288
  45.1 3.0 %collective-permute-start.7 = (f32[1,6,16,128]{3,2,1,0:T(8,128)S(1)}, f32[1,6,16,128]{3,2,1,0:T(8,128)S(1)}, u32[]{:S(2)}, u32[]{:S(2)}) collective-permute-start(f32[1,6,16,128]{3,2,1,0:T(8,128)S(1)} %collective-permute-done.5), channel_id=1, source_target_pairs={{0,224},{32,0},{64,32},{96,64},{128,96},{160,128},{192,160},{224,1... | collective-permute-start | bytes 147464 | tf_op jit(solution)/shard_map/ppermute | solution.py:206
  48.1 1.7 %collective-permute-done.6 = f32[1,6,16,128]{3,2,1,0:T(8,128)S(1)} collective-permute-done((f32[1,6,16,128]{3,2,1,0:T(8,128)S(1)}, f32[1,6,16,128]{3,2,1,0:T(8,128)S(1)}, u32[]{:S(2)}, u32[]{:S(2)}) %collective-permute-start.6) | collective-permute-done | bytes 49184 | tf_op jit(solution)/shard_map/ppermute | solution.py:199
  49.9 3.0 %collective-permute-start.9 = (f32[1,6,16,128]{3,2,1,0:T(8,128)S(1)}, f32[1,6,16,128]{3,2,1,0:T(8,128)S(1)}, u32[]{:S(2)}, u32[]{:S(2)}) collective-permute-start(f32[1,6,16,128]{3,2,1,0:T(8,128)S(1)} %collective-permute-done.7), channel_id=1, source_target_pairs={{0,224},{32,0},{64,32},{96,64},{128,96},{160,128},{192,160},{224,1... | collective-permute-start | bytes 147464 | tf_op jit(solution)/shard_map/ppermute | solution.py:206
  52.8 1.7 %collective-permute-done.8 = f32[1,6,16,128]{3,2,1,0:T(8,128)S(1)} collective-permute-done((f32[1,6,16,128]{3,2,1,0:T(8,128)S(1)}, f32[1,6,16,128]{3,2,1,0:T(8,128)S(1)}, u32[]{:S(2)}, u32[]{:S(2)}) %collective-permute-start.8) | collective-permute-done | bytes 49184 | tf_op jit(solution)/shard_map/ppermute | solution.py:199
  54.6 4.7 %collective-permute-done.10 = f32[1,6,16,128]{3,2,1,0:T(8,128)S(1)} collective-permute-done((f32[1,6,16,128]{3,2,1,0:T(8,128)S(1)}, f32[1,6,16,128]{3,2,1,0:T(8,128)S(1)}, u32[]{:S(2)}, u32[]{:S(2)}) %collective-permute-start.10) | collective-permute-done | bytes 49184 | tf_op jit(solution)/shard_map/ppermute | solution.py:199
  59.3 9.8 %all-to-all-start.1 = ((f32[32,1,2048]{2,1,0:T(1,128)}), f32[32,1,2048]{2,1,0:T(1,128)S(1)}, u32[]{:S(2)}, u32[]{:S(2)}) async-start(f32[32,1,2048]{2,1,0:T(1,128)} %reshape.57), calls=%async_computation.1 | async-start | bytes 524288 | tf_op jit(solution)/shard_map/all_to_all | solution.py:178
  69.2 0.4 while.40
  69.6 0.5 broadcast.610
  70.2 1.2 %reduce.1 = f32[32,2048]{1,0:T(8,128)S(1)} reduce(f32[32,1,2048]{2,1,0:T(1,128)S(1)} %all-to-all-done, f32[]{:T(128)} %broadcast.610), dimensions={1}, to_apply=%all_to_all.39.reduce_sub_computation | reduce | bytes 524292 | tf_op jit(solution)/shard_map/all_to_all | solution.py:177
  72.3 7.8 %all-to-all-done.1 = f32[32,1,2048]{2,1,0:T(1,128)S(1)} async-done(((f32[32,1,2048]{2,1,0:T(1,128)}), f32[32,1,2048]{2,1,0:T(1,128)S(1)}, u32[]{:S(2)}, u32[]{:S(2)}) %all-to-all-start.1) | async-done | bytes 262176 | tf_op jit(solution)/shard_map/all_to_all | solution.py:178
  80.1 1.2 %reduce = f32[32,2048]{1,0:T(8,128)S(1)} reduce(f32[32,1,2048]{2,1,0:T(1,128)S(1)} %all-to-all-done.1, f32[]{:T(128)} %broadcast.610), dimensions={1}, to_apply=%all_to_all.43.reduce_sub_computation | reduce | bytes 524292 | tf_op jit(solution)/shard_map/all_to_all | solution.py:178
  82.4 0.8 fusion.30
  83.1 0.7 fusion.35
  83.8 0.3 fusion.42
  84.2 0.6 fusion.47
  84.8 0.3 fusion.54
  85.1 0.6 fusion.59
  85.8 0.3 fusion.66
  86.1 0.6 fusion.71
  86.7 0.3 fusion.78
  87.1 0.6 fusion.83
  87.7 0.3 fusion.90
  88.0 0.6 fusion.95
  88.7 0.3 fusion.102
  89.0 0.3 fusion.107
  89.7 0.4 copy.176
  90.1 1.4 %reshape.59 = f32[32,1,2048]{2,1,0:T(1,128)} reshape(f32[512,4,32]{2,1,0:T(4,128)S(1)} %bitcast.134) | data formatting | bytes 524288
  91.5 4.5 %all-to-all-start.2 = ((f32[32,1,2048]{2,1,0:T(1,128)}), f32[32,1,2048]{2,1,0:T(1,128)S(1)}, u32[]{:S(2)}, u32[]{:S(2)}) async-start(f32[32,1,2048]{2,1,0:T(1,128)} %reshape.59), calls=%async_computation.2 | async-start | bytes 524288 | tf_op jit(solution)/shard_map/all_to_all | solution.py:185
  96.0 5.8 %while.41 = (s32[]{:T(128)}, f32[16,128]{1,0:T(8,128)S(1)}, f32[8,16,128]{2,1,0:T(8,128)S(1)}, f32[8,16,128]{2,1,0:T(8,128)S(1)}, f32[8,16,128]{2,1,0:T(8,128)},...) while((s32[]{:T(128)}, f32[16,128]{1,0:T(8,128)S(1)}, ...), condition=%wide.region_3.4_spmd.clone, body=%wide.region_2.3_spmd.clone.sunk | while | flops 10244 | bytes 65679 | solution.py:143
  96.0 0.7 bitcast_dynamic-update-slice_fusion.9
  96.8 0.7 bitcast_dynamic-update-slice_fusion.9
  97.5 0.7 bitcast_dynamic-update-slice_fusion.9
  98.2 0.7 bitcast_dynamic-update-slice_fusion.9
  98.9 0.7 bitcast_dynamic-update-slice_fusion.9
  99.7 0.7 bitcast_dynamic-update-slice_fusion.9
  100.4 0.7 bitcast_dynamic-update-slice_fusion.9
  101.1 0.7 bitcast_dynamic-update-slice_fusion.9
  101.9 5.1 %all-to-all-done.2 = f32[32,1,2048]{2,1,0:T(1,128)S(1)} async-done(((f32[32,1,2048]{2,1,0:T(1,128)}), f32[32,1,2048]{2,1,0:T(1,128)S(1)}, u32[]{:S(2)}, u32[]{:S(2)}) %all-to-all-start.2) | async-done | bytes 262176 | tf_op jit(solution)/shard_map/all_to_all | solution.py:185
  107.0 1.2 %reduce.2 = f32[32,2048]{1,0:T(8,128)S(1)} reduce(f32[32,1,2048]{2,1,0:T(1,128)S(1)} %all-to-all-done.2, f32[]{:T(128)} %broadcast.610), dimensions={1}, to_apply=%all_to_all.47.reduce_sub_computation | reduce | bytes 524292 | tf_op jit(solution)/shard_map/all_to_all | solution.py:185
  108.1 0.5 reshape.60
  108.9 0.4 copy.179
  109.4 0.5 copy-done.1
  110.1 0.5 fusion.324
  110.6 0.9 copy.189
  (111 shorter events, 8.5 us)
Async XLA Ops:
  0.7 18.3 %collective-permute-start.1 = (f32[2,16,128]{2,1,0:T(8,128)S(1)}, f32[2,16,128]{2,1,0:T(8,128)S(1)}, u32[]{:S(2)}, u32[]{:S(2)}) collective-permute-start(f32[2,16,128]{2,1,0:T(8,128)S(1)} %get-tuple-element.416), channel_id=1, source_target_pairs={{32,0},{64,32},{96,64},{128,96},{160,128},{192,160},{224,192},{33,... | collective-permute-start | bytes 49160 | tf_op jit(solution)/shard_map/ppermute | solution.py:18
  2.0 17.1 %collective-permute-start = (f32[2,16,128]{2,1,0:T(8,128)S(1)}, f32[2,16,128]{2,1,0:T(8,128)S(1)}, u32[]{:S(2)}, u32[]{:S(2)}) collective-permute-start(f32[2,16,128]{2,1,0:T(8,128)S(1)} %get-tuple-element.415), channel_id=1, source_target_pairs={{0,32},{32,64},{64,96},{96,128},{128,160},{160,192},{192,224},{1,3... | collective-permute-start | bytes 49160 | tf_op jit(solution)/shard_map/ppermute | solution.py:15
  7.7 11.4 %copy-start = (f32[32,16,128]{2,1,0:T(8,128)S(1)}, f32[32,16,128]{2,1,0:T(8,128)}, u32[]{:S(2)}) copy-start(f32[32,16,128]{2,1,0:T(8,128)} %param.5) | copy-start | bytes 786436
  7.7 51.6 %all-to-all-start = ((f32[32,1,2048]{2,1,0:T(1,128)}), f32[32,1,2048]{2,1,0:T(1,128)S(1)}, u32[]{:S(2)}, u32[]{:S(2)}) async-start(f32[32,1,2048]{2,1,0:T(1,128)} %reshape.55), calls=%async_computation | async-start | bytes 524288 | tf_op jit(solution)/shard_map/all_to_all | solution.py:177
  19.2 7.9 %collective-permute-start.2 = (f32[36,2,128]{2,0,1:T(8,128)S(1)}, f32[36,2,128]{2,0,1:T(8,128)S(1)}, u32[]{:S(2)}, u32[]{:S(2)}) collective-permute-start(f32[36,2,128]{2,0,1:T(8,128)S(1)} %copy.191), channel_id=1, source_target_pairs={{0,1},{1,2},{2,3},{3,4},{4,5},{5,6},{6,7},{7,8},{8,9},{9,10},{10,1... | collective-permute-start | bytes 110600 | tf_op jit(solution)/shard_map/ppermute | solution.py:15
  22.9 6.2 %collective-permute-start.3 = (f32[36,2,128]{2,0,1:T(8,128)S(1)}, f32[36,2,128]{2,0,1:T(8,128)S(1)}, u32[]{:S(2)}, u32[]{:S(2)}) collective-permute-start(f32[36,2,128]{2,0,1:T(8,128)S(1)} %copy.192), channel_id=1, source_target_pairs={{1,0},{2,1},{3,2},{4,3},{5,4},{6,5},{7,6},{8,7},{9,8},{10,9},{11,1... | collective-permute-start | bytes 110600 | tf_op jit(solution)/shard_map/ppermute | solution.py:18
  32.6 12.5 %collective-permute-start.4 = (f32[1,6,16,128]{3,2,1,0:T(8,128)S(1)}, f32[1,6,16,128]{3,2,1,0:T(8,128)S(1)}, u32[]{:S(2)}, u32[]{:S(2)}) collective-permute-start(f32[1,6,16,128]{3,2,1,0:T(8,128)S(1)} %bitcast.144), channel_id=1, source_target_pairs={{0,32},{32,64},{64,96},{96,128},{128,160},{160,192},{192,224},{224... | collective-permute-start | bytes 147464 | tf_op jit(solution)/shard_map/ppermute | solution.py:199
  32.7 12.5 %collective-permute-start.5 = (f32[1,6,16,128]{3,2,1,0:T(8,128)S(1)}, f32[1,6,16,128]{3,2,1,0:T(8,128)S(1)}, u32[]{:S(2)}, u32[]{:S(2)}) collective-permute-start(f32[1,6,16,128]{3,2,1,0:T(8,128)S(1)} %bitcast.145), channel_id=1, source_target_pairs={{0,224},{32,0},{64,32},{96,64},{128,96},{160,128},{192,160},{224,1... | collective-permute-start | bytes 147464 | tf_op jit(solution)/shard_map/ppermute | solution.py:206
  45.1 4.7 %collective-permute-start.6 = (f32[1,6,16,128]{3,2,1,0:T(8,128)S(1)}, f32[1,6,16,128]{3,2,1,0:T(8,128)S(1)}, u32[]{:S(2)}, u32[]{:S(2)}) collective-permute-start(f32[1,6,16,128]{3,2,1,0:T(8,128)S(1)} %collective-permute-done.4), channel_id=1, source_target_pairs={{0,32},{32,64},{64,96},{96,128},{128,160},{160,192},{192,224},{224... | collective-permute-start | bytes 147464 | tf_op jit(solution)/shard_map/ppermute | solution.py:199
  45.1 4.7 %collective-permute-start.7 = (f32[1,6,16,128]{3,2,1,0:T(8,128)S(1)}, f32[1,6,16,128]{3,2,1,0:T(8,128)S(1)}, u32[]{:S(2)}, u32[]{:S(2)}) collective-permute-start(f32[1,6,16,128]{3,2,1,0:T(8,128)S(1)} %collective-permute-done.5), channel_id=1, source_target_pairs={{0,224},{32,0},{64,32},{96,64},{128,96},{160,128},{192,160},{224,1... | collective-permute-start | bytes 147464 | tf_op jit(solution)/shard_map/ppermute | solution.py:206
  49.8 4.7 %collective-permute-start.8 = (f32[1,6,16,128]{3,2,1,0:T(8,128)S(1)}, f32[1,6,16,128]{3,2,1,0:T(8,128)S(1)}, u32[]{:S(2)}, u32[]{:S(2)}) collective-permute-start(f32[1,6,16,128]{3,2,1,0:T(8,128)S(1)} %collective-permute-done.6), channel_id=1, source_target_pairs={{0,32},{32,64},{64,96},{96,128},{128,160},{160,192},{192,224},{224... | collective-permute-start | bytes 147464 | tf_op jit(solution)/shard_map/ppermute | solution.py:199
  49.9 4.7 %collective-permute-start.9 = (f32[1,6,16,128]{3,2,1,0:T(8,128)S(1)}, f32[1,6,16,128]{3,2,1,0:T(8,128)S(1)}, u32[]{:S(2)}, u32[]{:S(2)}) collective-permute-start(f32[1,6,16,128]{3,2,1,0:T(8,128)S(1)} %collective-permute-done.7), channel_id=1, source_target_pairs={{0,224},{32,0},{64,32},{96,64},{128,96},{160,128},{192,160},{224,1... | collective-permute-start | bytes 147464 | tf_op jit(solution)/shard_map/ppermute | solution.py:206
  54.6 4.7 %collective-permute-start.10 = (f32[1,6,16,128]{3,2,1,0:T(8,128)S(1)}, f32[1,6,16,128]{3,2,1,0:T(8,128)S(1)}, u32[]{:S(2)}, u32[]{:S(2)}) collective-permute-start(f32[1,6,16,128]{3,2,1,0:T(8,128)S(1)} %collective-permute-done.8), channel_id=1, source_target_pairs={{0,32},{32,64},{64,96},{96,128},{128,160},{160,192},{192,224},{224... | collective-permute-start | bytes 147464 | tf_op jit(solution)/shard_map/ppermute | solution.py:199
  59.3 20.8 %all-to-all-start.1 = ((f32[32,1,2048]{2,1,0:T(1,128)}), f32[32,1,2048]{2,1,0:T(1,128)S(1)}, u32[]{:S(2)}, u32[]{:S(2)}) async-start(f32[32,1,2048]{2,1,0:T(1,128)} %reshape.57), calls=%async_computation.1 | async-start | bytes 524288 | tf_op jit(solution)/shard_map/all_to_all | solution.py:178
  69.6 1.7 %copy-start.5 = (f32[8,16,128]{2,1,0:T(8,128)}, f32[8,16,128]{2,1,0:T(8,128)S(1)}, u32[]{:S(2)}) copy-start(f32[8,16,128]{2,1,0:T(8,128)S(1)} %get-tuple-element.584) | copy-start | bytes 196612
  69.6 1.7 %copy-start.6 = (f32[8,16,128]{2,1,0:T(8,128)}, f32[8,16,128]{2,1,0:T(8,128)S(1)}, u32[]{:S(2)}) copy-start(f32[8,16,128]{2,1,0:T(8,128)S(1)} %get-tuple-element.586) | copy-start | bytes 196612
  91.5 15.5 %all-to-all-start.2 = ((f32[32,1,2048]{2,1,0:T(1,128)}), f32[32,1,2048]{2,1,0:T(1,128)S(1)}, u32[]{:S(2)}, u32[]{:S(2)}) async-start(f32[32,1,2048]{2,1,0:T(1,128)} %reshape.59), calls=%async_computation.2 | async-start | bytes 524288 | tf_op jit(solution)/shard_map/all_to_all | solution.py:185
  108.9 1.0 copy-start.1
  108.9 1.0 copy-start.2
  108.9 1.1 copy-start.3
  108.9 1.2 %copy-start.4 = (f32[32,16,128]{2,0,1:T(8,128)S(1)}, f32[32,16,128]{2,0,1:T(8,128)}, u32[]{:S(2)}) copy-start(f32[32,16,128]{2,0,1:T(8,128)} %get-tuple-element.309) | copy-start | bytes 786436
